TPU v7x, 32 devices: a whole 2x2x4 slice. The times are simulated.
32 devices in a mesh: mode: 16 (over z, y, x), real: 2 (over core).
Axes of the slice: x: 2, y: 2, z: 4, core: 2. Of those that a mesh axis runs over, the one named last changes fastest.
Arguments:
- input_field: bfloat16 [2, 2, 256, 16384], P(None, 'real', 'mode'), may hold values from -6 to 6
- kerr_coeff: bfloat16 [16, 64, 64], P('mode'), may hold values from -0.375 to 0.375
- block_list: int32 [16, 4], P('mode'), may hold values from 0 to 31
Outputs:
- density: float32 [512, 2, 256, 256], P('mode', None, 'real')
All inputs are finite; a program needn't handle non-finite values.
Results may differ from a plain program's by a relative error of at most 0.0085.
Values may be sent and summed in bfloat16 or wider, within the bound.
A program may use at most 64 MiB of HBM per device.

v0:
```python
import functools
import math

import jax
import jax.numpy as jnp
import numpy as np
from jax import lax
from jax.experimental import pallas as pl
from jax.experimental.pallas import tpu as pltpu
from jax.sharding import PartitionSpec as P

MB = 8
FT = 128
NT = 16384
FB = 32


kerr_strength = 0.25


def kerr_terms(field_blocks, coeff_group, block_group):
    mode_l = jnp.take(field_blocks, block_group[:, 1], axis=2).astype(jnp.float32)
    mode_m = jnp.take(field_blocks, block_group[:, 2], axis=2).astype(jnp.float32)
    mode_n = jnp.take(field_blocks, block_group[:, 3], axis=2).astype(jnp.float32)
    realiz = field_blocks.shape[1]
    group_size = block_group.shape[0]
    steps_local = field_blocks.shape[4]
    prod_re = (
        mode_m[0][:, :, :, None, :] * mode_n[0][:, :, None, :, :]
        + mode_m[1][:, :, :, None, :] * mode_n[1][:, :, None, :, :]
    )
    prod_im = (
        mode_m[1][:, :, :, None, :] * mode_n[0][:, :, None, :, :]
        - mode_m[0][:, :, :, None, :] * mode_n[1][:, :, None, :, :]
    )
    pairs = (
        jnp.stack([prod_re, prod_im])
        .reshape(2, realiz, group_size, MB * MB, steps_local)
        .astype(jnp.bfloat16)
    )
    weighted = jnp.einsum(
        "kab,crkbt->crkat", coeff_group, pairs, preferred_element_type=jnp.float32
    )
    weighted = weighted.reshape(2, realiz, group_size, MB, MB, steps_local)
    term_re = jnp.sum(
        weighted[0] * mode_l[0][:, :, None] - weighted[1] * mode_l[1][:, :, None], axis=3
    )
    term_im = jnp.sum(
        weighted[0] * mode_l[1][:, :, None] + weighted[1] * mode_l[0][:, :, None], axis=3
    )
    one_hot = (
        block_group[:, 0][:, None] == jnp.arange(field_blocks.shape[2], dtype=jnp.int32)[None, :]
    ).astype(jnp.float32)
    return jnp.einsum(
        "kg,crkpt->crgpt", one_hot, jnp.stack([term_re, term_im]), precision=lax.Precision.HIGHEST
    )


def phase_table(extent, modulus):
    index_a = jnp.arange(extent, dtype=jnp.int32)[:, None]
    index_b = jnp.arange(extent, dtype=jnp.int32)[None, :]
    angle = 2.0 * math.pi / modulus * (index_a * index_b % modulus).astype(jnp.float32)
    return (jnp.cos(angle), -jnp.sin(angle))


def first_pass(table, data):
    table_high = table.astype(jnp.bfloat16)
    table_low = (table - table_high.astype(jnp.float32)).astype(jnp.bfloat16)
    upper = jnp.einsum("kn,rmnj->rmkj", table_high, data, preferred_element_type=jnp.float32)
    return upper + jnp.einsum("kn,rmnj->rmkj", table_low, data, preferred_element_type=jnp.float32)


def second_pass(table, data):
    return jnp.einsum("jn,rmkn->rmjk", table, data, precision=lax.Precision.HIGH)


def transform(by_mode):
    realiz = by_mode.shape[1]
    local_modes = by_mode.shape[2]
    signal = by_mode.reshape(2, realiz, local_modes, FT, FT)
    four_re, four_im = phase_table(FT, FT)
    twist_re, twist_im = phase_table(FT, NT)
    half_re = first_pass(four_re, signal[0]) - first_pass(four_im, signal[1])
    half_im = first_pass(four_re, signal[1]) + first_pass(four_im, signal[0])
    turned_re = half_re * twist_re - half_im * twist_im
    turned_im = half_re * twist_im + half_im * twist_re
    out_re = (second_pass(four_re, turned_re) - second_pass(four_im, turned_im)) / FT
    out_im = (second_pass(four_re, turned_im) + second_pass(four_im, turned_re)) / FT
    return jnp.stack([out_re, out_im]).astype(jnp.bfloat16)


def gram_parts(rows_part, cols_part):
    mode_parts = jnp.einsum(
        "crpbf,drqbf->bcdpq", rows_part, cols_part, preferred_element_type=jnp.float32
    )
    return jnp.stack(
        [mode_parts[:, 0, 0] + mode_parts[:, 1, 1], mode_parts[:, 1, 0] - mode_parts[:, 0, 1]], axis=1
    )


def shards(input_field, kerr_coeff, block_list):
    timed = lax.all_to_all(input_field, "mode", split_axis=3, concat_axis=2, tiled=True)
    realiz = timed.shape[1]
    width = timed.shape[2]
    steps_local = timed.shape[3]
    field_blocks = timed.reshape(2, realiz, width // MB, MB, steps_local)
    initial = jnp.zeros(field_blocks.shape, jnp.float32)
    running = initial
    coeff_piece = lax.all_gather(kerr_coeff, "mode", axis=0, tiled=True)
    block_piece = lax.all_gather(block_list, "mode", axis=0, tiled=True)
    block_count = block_piece.shape[0]
    coeff_groups = coeff_piece.reshape(
        block_count // 8, 8, coeff_piece.shape[1], coeff_piece.shape[2]
    )
    block_groups = block_piece.reshape(block_count // 8, 8, 4)

    def one_group(carried, groups):
        return (carried + kerr_terms(field_blocks, groups[0], groups[1]), None)

    running, unused = lax.scan(one_group, running, (coeff_groups, block_groups))
    kerr_sum = running
    kerr_sum = kerr_sum.reshape(2, realiz, width, steps_local)
    base = timed.astype(jnp.float32)
    stepped = jnp.stack(
        [base[0] - kerr_strength * kerr_sum[1], base[1] + kerr_strength * kerr_sum[0]]
    ).astype(jnp.bfloat16)
    by_mode = lax.all_to_all(stepped, "mode", split_axis=2, concat_axis=3, tiled=True)
    spectrum = transform(by_mode)
    banded = lax.all_to_all(spectrum, "mode", split_axis=3, concat_axis=2, tiled=True)
    bands_dev = banded.shape[3] * FT // FB
    spec_bands = banded.reshape(2, realiz, width, bands_dev, FB)
    scale = 1.0 / (FB * realiz * lax.axis_size("real"))
    row_count = width // lax.axis_size("real")
    row_first = lax.axis_index("real") * row_count
    shard_piece = lax.all_gather(spec_bands, "real", axis=1, tiled=True)
    own_part = lax.dynamic_slice_in_dim(shard_piece, row_first, row_count, 2)
    return gram_parts(own_part, shard_piece) * scale


VMEM = pltpu.VMEM
BIG = 60 * 1024 * 1024


def step_order(parts):
    return sorted(range(1, parts), key=lambda step: (-min(step, parts - step), step))


def remote(here, there, sent, landed, target):
    copy = pltpu.make_async_remote_copy(
        src_ref=here,
        dst_ref=there,
        send_sem=sent,
        recv_sem=landed,
        device_id=target,
        device_id_type=pl.DeviceIdType.MESH,
    )
    copy.start()
    return copy


def kerr_terms_at(first, piece, k, list_s, coef, fld, terms):
    span = pl.ds(first, piece)
    bl, bm, bn = (list_s[k, 0, i] for i in (1, 2, 3))
    m_re, m_im = fld[0, bm, :, span][:, None], fld[1, bm, :, span][:, None]
    n_re, n_im = fld[0, bn, :, span][None], fld[1, bn, :, span][None]
    p_re = (m_re * n_re + m_im * n_im).reshape(MB * MB, piece)
    p_im = (m_im * n_re - m_re * n_im).reshape(MB * MB, piece)
    pairs = jnp.concatenate([p_re, p_im], axis=1).astype(jnp.bfloat16)
    w = jnp.dot(coef, pairs, preferred_element_type=jnp.float32)
    w_re = w[:, :piece].reshape(MB, MB, piece)
    w_im = w[:, piece:].reshape(MB, MB, piece)
    l_re, l_im = fld[0, bl, :, span][:, None], fld[1, bl, :, span][:, None]
    at = pl.ds(pl.multiple_of(k * MB, MB), MB)
    terms[0, at, span] = jnp.sum(w_re * l_re - w_im * l_im, axis=0)
    terms[1, at, span] = jnp.sum(w_re * l_im + w_im * l_re, axis=0)


def owner_table(blocks, width, list_s):
    shape = (width, blocks * MB)
    row = lax.broadcasted_iota(jnp.int32, shape, 0)
    col = lax.broadcasted_iota(jnp.int32, shape, 1)
    wanted = jnp.full(shape, -1, jnp.int32)
    for k in range(blocks):
        wanted = jnp.where(col // MB == k, list_s[k, 0, 0] * MB + col % MB, wanted)
    return (row == wanted).astype(jnp.float32).astype(jnp.bfloat16)


def whole_kernel(parts, sides, x_ref, coef_ref, list_ref, f1h, f1l, tw_re, tw_im, f2h, f2l,
                 out_ref, timed, coefs, swapped, lists, list_s, fld, terms, rows, stepped, by_mode, spec,
                 sends, recvs, own_sems):
    me = lax.axis_index("mode")
    other = {"real": 1 - lax.axis_index("real")}
    _, modes, times = x_ref.shape
    steps = times // parts
    width = parts * modes
    groups = width // MB
    fine = steps // FT
    pieces = min(2, fine)
    half = steps // pieces
    piece = min(half, 256)
    order = step_order(parts)
    barrier = pltpu.get_barrier_semaphore()
    for step in order:
        to = {"mode": lax.rem(me + step, parts)}
        pl.semaphore_signal(barrier, inc=1, device_id=to, device_id_type=pl.DeviceIdType.MESH)
    if sides > 1:
        pl.semaphore_signal(barrier, inc=1, device_id=other, device_id_type=pl.DeviceIdType.MESH)
    pl.semaphore_wait(barrier, parts - 1 + (sides > 1))

    def chunk(to, part):
        at = pl.multiple_of(to * steps + part * half, 128)
        return x_ref.at[:, :, pl.ds(at, half)]

    def landing(part):
        return timed.at[me, :, :, pl.ds(part * half, half)]

    small, field_copies = [], [[] for _ in range(pieces)]
    for step in order:
        to = lax.rem(me + step, parts)
        there = {"mode": to}
        small.append(remote(coef_ref, coefs.at[me], sends.at[0, step], recvs.at[0, step], there))
        small.append(remote(list_ref, lists.at[me], sends.at[1, step], recvs.at[1, step], there))
    for part, copies in enumerate(field_copies):
        for step in order:
            to = lax.rem(me + step, parts)
            copies.append(
                remote(
                    chunk(to, part),
                    landing(part),
                    sends.at[4 + part, step],
                    recvs.at[4 + part, step],
                    {"mode": to},
                )
            )
    for slot, (here, there) in enumerate(((coef_ref, coefs.at[me]), (list_ref, lists.at[me]))):
        copy = pltpu.make_async_copy(here, there, own_sems.at[slot])
        copy.start()
        small.append(copy)
    for part, copies in enumerate(field_copies):
        copy = pltpu.make_async_copy(chunk(me, part), landing(part), own_sems.at[4 + part])
        copy.start()
        copies.append(copy)
    for copy in small:
        copy.wait()
    copy = pltpu.make_async_copy(lists, list_s, own_sems.at[2])
    copy.start()
    copy.wait()
    blocks = coefs.shape[0]
    owners = owner_table(blocks, width, list_s)
    order_of = (MB * MB, MB * MB)
    row = lax.broadcasted_iota(jnp.int32, order_of, 0)
    col = lax.broadcasted_iota(jnp.int32, order_of, 1)
    swap = (col == (row % MB) * MB + row // MB).astype(jnp.float32).astype(jnp.bfloat16)
    for k in range(blocks):
        swapped[k] = jnp.dot(
            swap, coefs[k], preferred_element_type=jnp.float32
        ).astype(jnp.bfloat16)
    for part, copies in enumerate(field_copies):
        for copy in copies:
            copy.wait()
        span = pl.ds(part * half, half)
        for c in range(2):
            fld[c, :, :, span] = timed[:, c, :, span].astype(jnp.float32).reshape(groups, MB, half)

        def one_block(k, carry):
            coef = swapped[k]
            for at in range(part * half, (part + 1) * half, piece):
                kerr_terms_at(at, piece, k, list_s, coef, fld, terms)
            return carry

        lax.fori_loop(0, blocks, one_block, 0, unroll=2)
        for c in range(2):
            term = terms[1 - c, :, span]
            high = term.astype(jnp.bfloat16)
            low = (term - high.astype(jnp.float32)).astype(jnp.bfloat16)
            kerr = jnp.dot(owners, high, preferred_element_type=jnp.float32)
            kerr = kerr + jnp.dot(owners, low, preferred_element_type=jnp.float32)
            turn = kerr_strength * (2 * c - 1)
            new = fld[c, :, :, span].reshape(width, half) + turn * kerr
            for g in range(groups):
                for n in range(half // FT):
                    row = g * (MB * 2 * fine) + c * fine + part * (half // FT) + n
                    rows[pl.ds(row, MB, stride=2 * fine), :] = new[
                        g * MB : (g + 1) * MB, n * FT : (n + 1) * FT
                    ]
    stepped[...] = rows[...].astype(jnp.bfloat16).reshape(stepped.shape)

    mode_parts = min(2, modes // 2)
    few = modes // mode_parts
    mode_copies = []
    for part in range(mode_parts):
        some = pl.ds(part * few, few)
        copies = []
        for step in order:
            to = lax.rem(me + step, parts)
            copies.append(
                remote(
                    stepped.at[to, some],
                    by_mode.at[me, some],
                    sends.at[8 + part, step],
                    recvs.at[8 + part, step],
                    {"mode": to},
                )
            )
        copy = pltpu.make_async_copy(
            stepped.at[me, some], by_mode.at[me, some], own_sems.at[8 + part]
        )
        copy.start()
        mode_copies.append(copies + [copy])
    for part, copies in enumerate(mode_copies):
        for copy in copies:
            copy.wait()
        some = range(part * few, (part + 1) * few)
        dft_modes(some, by_mode, f1h, f1l, tw_re, tw_im, f2h, f2l, rows)
    spec[...] = rows[...].astype(jnp.bfloat16).reshape(spec.shape)

    pending, passed = [], []
    for step in order:
        to = lax.rem(me + step, parts)
        pending.append(
            (
                remote(spec.at[to], out_ref.at[0, me], sends.at[2, step], recvs.at[2, step], {"mode": to}),
                lax.rem(me - step + parts, parts),
            )
        )
    copy = pltpu.make_async_copy(spec.at[me], out_ref.at[0, me], own_sems.at[3])
    copy.start()
    if sides > 1:
        passed.append(remote(spec.at[me], out_ref.at[1, me], sends.at[3, 0], recvs.at[3, 0], other))
    for step, (arrival, source) in zip(order, pending):
        arrival.wait_recv()
        if sides > 1:
            passed.append(
                remote(
                    out_ref.at[0, source],
                    out_ref.at[1, source],
                    sends.at[3, step],
                    recvs.at[3, step],
                    other,
                )
            )
    copy.wait()
    for arrival, _ in pending:
        arrival.wait_send()
    for copy in passed:
        copy.wait()


def spectra_of(field, coef, listed, parts, sides):
    _, modes, times = field.shape
    steps = times // parts
    width = parts * modes
    fine = steps // FT
    half = jnp.bfloat16
    return pl.pallas_call(
        functools.partial(whole_kernel, parts, sides),
        out_shape=jax.ShapeDtypeStruct((sides, parts, fine, 2, modes, FT), half),
        in_specs=[pl.BlockSpec(memory_space=pl.ANY)] + [pl.BlockSpec(memory_space=VMEM)] * 8,
        out_specs=pl.BlockSpec(memory_space=VMEM),
        scratch_shapes=[
            VMEM((parts, 2, modes, steps), half),
            VMEM((parts,) + coef.shape, half),
            VMEM((parts,) + coef.shape, half),
            VMEM((parts,) + listed.shape, jnp.int32),
            pltpu.SMEM((parts,) + listed.shape, jnp.int32),
            VMEM((2, width // MB, MB, steps), jnp.float32),
            VMEM((2, parts * MB, steps), jnp.float32),
            VMEM((2 * width * fine, FT), jnp.float32),
            VMEM((parts, modes, 2 * fine, FT), half),
            VMEM((parts, modes, 2 * fine, FT), half),
            VMEM((parts, fine, 2, modes, FT), half),
            pltpu.SemaphoreType.DMA((12, parts)),
            pltpu.SemaphoreType.DMA((12, parts)),
            pltpu.SemaphoreType.DMA((12,)),
        ],
        compiler_params=pltpu.CompilerParams(
            collective_id=0, has_side_effects=True, vmem_limit_bytes=BIG
        ),
    )(field, coef, listed, *dft_tables(parts))


def dft_tables(parts):
    a = np.arange(FT)
    four = np.exp(-2j * np.pi / FT * (np.outer(a, a) % FT))
    twist = np.exp(-2j * np.pi / NT * (np.outer(a, a) % NT)) / FT
    real = np.block([[four.real, -four.imag], [four.imag, four.real]])
    first = real.reshape(2 * FT, 2, parts, FT // parts).transpose(0, 2, 1, 3)
    first = first.reshape(2 * FT, 2 * FT)
    second = real.reshape(2, FT, 2 * FT).transpose(1, 0, 2).reshape(2 * FT, 2 * FT)

    def split(t):
        t = t.astype(np.float32)
        high = t.astype(jnp.bfloat16)
        return high, (t - high.astype(np.float32)).astype(jnp.bfloat16)

    return (
        *split(first),
        twist.real.astype(np.float32),
        twist.imag.astype(np.float32),
        *split(second),
    )


def dft_modes(some, x_ref, f1h, f1l, tw_re, tw_im, f2h, f2l, rows):
    modes = x_ref.shape[1]
    nt = (((1,), (1,)), ((), ()))
    dot = functools.partial(jnp.dot, preferred_element_type=jnp.float32)
    dot_nt = functools.partial(
        lax.dot_general, dimension_numbers=nt, preferred_element_type=jnp.float32
    )
    for m in some[::2]:
        x = jnp.concatenate(
            [x_ref[:, m].reshape(2 * FT, FT), x_ref[:, m + 1].reshape(2 * FT, FT)], axis=1
        )
        half = dot(f1h[...], x) + dot(f1l[...], x)
        turned = []
        for i in range(2):
            h_re, h_im = half[:FT, i * FT : (i + 1) * FT], half[FT:, i * FT : (i + 1) * FT]
            turned.append(
                jnp.concatenate(
                    [
                        h_re * tw_re[...] - h_im * tw_im[...],
                        h_re * tw_im[...] + h_im * tw_re[...],
                    ],
                    axis=1,
                )
            )
        turned = jnp.concatenate(turned, axis=0)
        high = turned.astype(jnp.bfloat16)
        low = (turned - high.astype(jnp.float32)).astype(jnp.bfloat16)
        out = dot_nt(f2h[...], high) + dot_nt(f2h[...], low) + dot_nt(f2l[...], high)
        for i in range(2):
            rows[pl.ds(m + i, 2 * FT, stride=modes), :] = out[:, i * FT : (i + 1) * FT]


def gram_kernel(scale, half_ref, spec_ref, out_ref):
    sides, parts, _, _, modes, _ = spec_ref.shape
    row_count = out_ref.shape[2]
    sources = row_count // modes
    first = half_ref[0] * sources
    cols, rows_re, rows_im = [], [], []
    for side in range(sides):
        re, im = (spec_ref[side, :, 0, c].reshape(parts * modes, FT) for c in range(2))
        own = pl.ds(first, sources)
        own_re, own_im = (spec_ref[side, own, 0, c].reshape(row_count, FT) for c in range(2))
        cols += [re, im]
        rows_re += [own_re, own_im]
        rows_im += [own_im, -own_re]
    cols = jnp.concatenate(cols, axis=1)
    rows = jnp.concatenate(
        [jnp.concatenate(rows_re, axis=1), jnp.concatenate(rows_im, axis=1)], axis=0
    )
    lane = lax.broadcasted_iota(jnp.int32, rows.shape, 1)
    band = (lane % FT) // FB
    for g in range(FT // FB):
        kept = jnp.where(band == g, rows, jnp.zeros_like(rows))
        out = lax.dot_general(
            kept, cols, (((1,), (1,)), ((), ())), preferred_element_type=jnp.float32
        )
        out_ref[g] = (out * scale).reshape(2, row_count, parts * modes)


def gram(half, spectra, row_count, scale):
    sides, parts, high, _, modes, _ = spectra.shape
    width = parts * modes
    per = FT // FB
    return pl.pallas_call(
        functools.partial(gram_kernel, scale),
        grid=(high,),
        out_shape=jax.ShapeDtypeStruct((high * per, 2, row_count, width), jnp.float32),
        in_specs=[
            pl.BlockSpec(memory_space=pltpu.SMEM),
            pl.BlockSpec((sides, parts, 1, 2, modes, FT), lambda j: (0, 0, j, 0, 0, 0)),
        ],
        out_specs=pl.BlockSpec((per, 2, row_count, width), lambda j: (j, 0, 0, 0)),
        compiler_params=pltpu.CompilerParams(vmem_limit_bytes=BIG),
    )(half, spectra)


def tiled_shards(input_field, kerr_coeff, block_list):
    parts, sides = lax.axis_size("mode"), lax.axis_size("real")
    _, _, modes, times = input_field.shape
    width = parts * modes
    spectra = spectra_of(
        input_field.reshape(2, modes, times), kerr_coeff[0], block_list, parts, sides
    )
    half = lax.axis_index("real").astype(jnp.int32).reshape(1)
    return gram(half, spectra, width // sides, 1.0 / (FB * sides))


def tiles_fit(mesh):
    parts = mesh.shape["mode"]
    return FT % parts == 0 and (2 * FT // parts) % 16 == 0 and mesh.shape["real"] <= 2


def either(mesh, input_field, kerr_coeff, block_list):
    modes = input_field.shape[2]
    blocks_each = kerr_coeff.shape[0]
    fits = tiles_fit(mesh) and modes % 16 == 0 and blocks_each == 1
    fits = fits and input_field.shape[1] == 1 and input_field.shape[3] == NT
    return (tiled_shards if fits else shards)(input_field, kerr_coeff, block_list)


def solution(mesh):
    return jax.shard_map(
        functools.partial(either, mesh),
        mesh=mesh,
        in_specs=(P(None, "real", "mode", None), P("mode", None, None), P("mode", None)),
        out_specs=P("mode", None, "real", None),
        check_vma=False,
    )
```

profile of v0, /device:TPU:0, one launch (start us, length us, event | category | flops | bytes accessed | tf_op | source)
XLA Modules:
  0.0 101.1 jit_solution(1837882840755797653)
XLA Ops:
  0.0 92.8 %shard_map.91.spec_ref = bf16[2,16,8,2,16,128]{5,4,3,2,1,0:T(8,128)(2,1)} custom-call(bf16[2,16,16384]{2,1,0:T(8,128)(2,1)} %bitcast.3, bf16[64,64]{1,0:T(8,128)(2,1)} %bitcast.4, s32[1,4]{1,0:T(1,128)} %list_ref.1, bf16[256,256]{1,0:T(8,128)(2,1)} %constant.16.clone.f1h, bf16[256,256]{1,0:T(8,128)(2,1)} %constant.17.clone.f1l, ...), custom_call_target="tpu_custom_call" | custom-call | tf_op jit(solution)/shard_map/pallas_call | solution.py:355
  92.8 8.3 %shard_map.92 = f32[32,2,128,256]{3,2,1,0:T(8,128)} custom-call(s32[1]{0:T(128)} %bitcast.half_ref, bf16[2,16,8,2,16,128]{5,4,3,2,1,0:T(8,128)(2,1)} %shard_map.91.spec_ref), custom_call_target="tpu_custom_call" | custom-call | tf_op jit(solution)/shard_map/pallas_call | solution.py:467
where the time goes:
time: 101 us
  Pallas kernels  101 us (100%)
    pallas_call x1, Pallas kernels, spectra_of(): pl.pallas_call(functools.partial(whole_kernel, parts, sides), out_shape=j...  92.8 us
    pallas_call x1, Pallas kernels, gram(): pl.pallas_call(functools.partial(gram_kernel, scale), grid=(high,), out_s...  8.32 us

commit v1 on v0

v1 whole, which is shorter than its diff:
```python
import functools
import math

import jax
import jax.numpy as jnp
import numpy as np
from jax import lax
from jax.experimental import pallas as pl
from jax.experimental.pallas import tpu as pltpu
from jax.sharding import PartitionSpec as P

MB = 8
FT = 128
NT = 16384
FB = 32


kerr_strength = 0.25


def kerr_terms(field_blocks, coeff_group, block_group):
    mode_l = jnp.take(field_blocks, block_group[:, 1], axis=2).astype(jnp.float32)
    mode_m = jnp.take(field_blocks, block_group[:, 2], axis=2).astype(jnp.float32)
    mode_n = jnp.take(field_blocks, block_group[:, 3], axis=2).astype(jnp.float32)
    realiz = field_blocks.shape[1]
    group_size = block_group.shape[0]
    steps_local = field_blocks.shape[4]
    prod_re = (
        mode_m[0][:, :, :, None, :] * mode_n[0][:, :, None, :, :]
        + mode_m[1][:, :, :, None, :] * mode_n[1][:, :, None, :, :]
    )
    prod_im = (
        mode_m[1][:, :, :, None, :] * mode_n[0][:, :, None, :, :]
        - mode_m[0][:, :, :, None, :] * mode_n[1][:, :, None, :, :]
    )
    pairs = (
        jnp.stack([prod_re, prod_im])
        .reshape(2, realiz, group_size, MB * MB, steps_local)
        .astype(jnp.bfloat16)
    )
    weighted = jnp.einsum(
        "kab,crkbt->crkat", coeff_group, pairs, preferred_element_type=jnp.float32
    )
    weighted = weighted.reshape(2, realiz, group_size, MB, MB, steps_local)
    term_re = jnp.sum(
        weighted[0] * mode_l[0][:, :, None] - weighted[1] * mode_l[1][:, :, None], axis=3
    )
    term_im = jnp.sum(
        weighted[0] * mode_l[1][:, :, None] + weighted[1] * mode_l[0][:, :, None], axis=3
    )
    one_hot = (
        block_group[:, 0][:, None] == jnp.arange(field_blocks.shape[2], dtype=jnp.int32)[None, :]
    ).astype(jnp.float32)
    return jnp.einsum(
        "kg,crkpt->crgpt", one_hot, jnp.stack([term_re, term_im]), precision=lax.Precision.HIGHEST
    )


def phase_table(extent, modulus):
    index_a = jnp.arange(extent, dtype=jnp.int32)[:, None]
    index_b = jnp.arange(extent, dtype=jnp.int32)[None, :]
    angle = 2.0 * math.pi / modulus * (index_a * index_b % modulus).astype(jnp.float32)
    return (jnp.cos(angle), -jnp.sin(angle))


def first_pass(table, data):
    table_high = table.astype(jnp.bfloat16)
    table_low = (table - table_high.astype(jnp.float32)).astype(jnp.bfloat16)
    upper = jnp.einsum("kn,rmnj->rmkj", table_high, data, preferred_element_type=jnp.float32)
    return upper + jnp.einsum("kn,rmnj->rmkj", table_low, data, preferred_element_type=jnp.float32)


def second_pass(table, data):
    return jnp.einsum("jn,rmkn->rmjk", table, data, precision=lax.Precision.HIGH)


def transform(by_mode):
    realiz = by_mode.shape[1]
    local_modes = by_mode.shape[2]
    signal = by_mode.reshape(2, realiz, local_modes, FT, FT)
    four_re, four_im = phase_table(FT, FT)
    twist_re, twist_im = phase_table(FT, NT)
    half_re = first_pass(four_re, signal[0]) - first_pass(four_im, signal[1])
    half_im = first_pass(four_re, signal[1]) + first_pass(four_im, signal[0])
    turned_re = half_re * twist_re - half_im * twist_im
    turned_im = half_re * twist_im + half_im * twist_re
    out_re = (second_pass(four_re, turned_re) - second_pass(four_im, turned_im)) / FT
    out_im = (second_pass(four_re, turned_im) + second_pass(four_im, turned_re)) / FT
    return jnp.stack([out_re, out_im]).astype(jnp.bfloat16)


def gram_parts(rows_part, cols_part):
    mode_parts = jnp.einsum(
        "crpbf,drqbf->bcdpq", rows_part, cols_part, preferred_element_type=jnp.float32
    )
    return jnp.stack(
        [mode_parts[:, 0, 0] + mode_parts[:, 1, 1], mode_parts[:, 1, 0] - mode_parts[:, 0, 1]], axis=1
    )


def shards(input_field, kerr_coeff, block_list):
    timed = lax.all_to_all(input_field, "mode", split_axis=3, concat_axis=2, tiled=True)
    realiz = timed.shape[1]
    width = timed.shape[2]
    steps_local = timed.shape[3]
    field_blocks = timed.reshape(2, realiz, width // MB, MB, steps_local)
    initial = jnp.zeros(field_blocks.shape, jnp.float32)
    running = initial
    coeff_piece = lax.all_gather(kerr_coeff, "mode", axis=0, tiled=True)
    block_piece = lax.all_gather(block_list, "mode", axis=0, tiled=True)
    block_count = block_piece.shape[0]
    coeff_groups = coeff_piece.reshape(
        block_count // 8, 8, coeff_piece.shape[1], coeff_piece.shape[2]
    )
    block_groups = block_piece.reshape(block_count // 8, 8, 4)

    def one_group(carried, groups):
        return (carried + kerr_terms(field_blocks, groups[0], groups[1]), None)

    running, unused = lax.scan(one_group, running, (coeff_groups, block_groups))
    kerr_sum = running
    kerr_sum = kerr_sum.reshape(2, realiz, width, steps_local)
    base = timed.astype(jnp.float32)
    stepped = jnp.stack(
        [base[0] - kerr_strength * kerr_sum[1], base[1] + kerr_strength * kerr_sum[0]]
    ).astype(jnp.bfloat16)
    by_mode = lax.all_to_all(stepped, "mode", split_axis=2, concat_axis=3, tiled=True)
    spectrum = transform(by_mode)
    banded = lax.all_to_all(spectrum, "mode", split_axis=3, concat_axis=2, tiled=True)
    bands_dev = banded.shape[3] * FT // FB
    spec_bands = banded.reshape(2, realiz, width, bands_dev, FB)
    scale = 1.0 / (FB * realiz * lax.axis_size("real"))
    row_count = width // lax.axis_size("real")
    row_first = lax.axis_index("real") * row_count
    shard_piece = lax.all_gather(spec_bands, "real", axis=1, tiled=True)
    own_part = lax.dynamic_slice_in_dim(shard_piece, row_first, row_count, 2)
    return gram_parts(own_part, shard_piece) * scale


VMEM = pltpu.VMEM
ANY = pl.ANY
HALF = jnp.bfloat16
SUB = 8


def plane_size(parts):
    return 4 if parts % 4 == 0 else 1


def partner_order(parts):
    plane = plane_size(parts)
    return sorted(range(1, parts), key=lambda step: (-(step // plane), step))


def partner(me, step):
    to, bit = me, 1
    while bit <= step:
        if step & bit:
            to = to + bit - 2 * bit * (me // bit % 2)
        bit *= 2
    return to


def remote(here, there, sent, landed, target):
    copy = pltpu.make_async_remote_copy(
        src_ref=here,
        dst_ref=there,
        send_sem=sent,
        recv_sem=landed,
        device_id=target,
        device_id_type=pl.DeviceIdType.MESH,
    )
    copy.start()
    return copy


def local(here, there, sem):
    copy = pltpu.make_async_copy(here, there, sem)
    copy.start()
    return copy


def kerr_terms_of(k, list_s, coef, fld, terms):
    piece = fld.shape[3]
    bl, bm, bn = (list_s[k, 0, i] for i in (1, 2, 3))
    m_re, m_im = fld[0, bm][:, None], fld[1, bm][:, None]
    n_re, n_im = fld[0, bn][None], fld[1, bn][None]
    p_re = (m_re * n_re + m_im * n_im).reshape(MB * MB, piece)
    p_im = (m_im * n_re - m_re * n_im).reshape(MB * MB, piece)
    pairs = jnp.concatenate([p_re, p_im], axis=1).astype(HALF)
    w = jnp.dot(coef, pairs, preferred_element_type=jnp.float32)
    w_re = w[:, :piece].reshape(MB, MB, piece)
    w_im = w[:, piece:].reshape(MB, MB, piece)
    l_re, l_im = fld[0, bl][:, None], fld[1, bl][:, None]
    at = pl.ds(pl.multiple_of(k * MB, MB), MB)
    terms[0, at] = jnp.sum(w_re * l_re - w_im * l_im, axis=0)
    terms[1, at] = jnp.sum(w_re * l_im + w_im * l_re, axis=0)


def owner_table(blocks, width, list_s):
    shape = (width, blocks * MB)
    row = lax.broadcasted_iota(jnp.int32, shape, 0)
    col = lax.broadcasted_iota(jnp.int32, shape, 1)
    wanted = jnp.full(shape, -1, jnp.int32)
    for k in range(blocks):
        wanted = jnp.where(col // MB == k, list_s[k, 0, 0] * MB + col % MB, wanted)
    return (row == wanted).astype(jnp.float32).astype(HALF)


def swap_rows(coef):
    order_of = (MB * MB, MB * MB)
    row = lax.broadcasted_iota(jnp.int32, order_of, 0)
    col = lax.broadcasted_iota(jnp.int32, order_of, 1)
    swap = (col == (row % MB) * MB + row // MB).astype(jnp.float32).astype(HALF)
    return jnp.dot(swap, coef, preferred_element_type=jnp.float32).astype(HALF)


def pack_coef(coef):
    rows = coef.shape[0] // 2
    return jnp.concatenate([coef[:rows], coef[rows:]], axis=1)


def unpack_coef(packed):
    lanes = packed.shape[1] // 2
    return jnp.concatenate([packed[:, :lanes], packed[:, lanes:]], axis=0)


def whole_kernel(parts, sides, pieces, x_ref, coef_ref, list_ref, *refs):
    table_refs, out_ref = refs[:6], refs[6]
    (timed, coef_in, coef_own, coefs, lists, list_s, fld, terms, stepped, by_mode, xf, rows, spec) = refs[7:20]
    tables, (sends, recvs, own_sems) = refs[20:26], refs[26:]
    me = lax.axis_index("mode")
    other = {"real": 1 - lax.axis_index("real")}
    _, modes, times = x_ref.shape
    steps = times // parts
    width = parts * modes
    groups = width // MB
    half = steps // pieces
    tiles = half // FT
    fine = steps // FT
    halves = modes // SUB
    order = partner_order(parts)
    plane = plane_size(parts)
    barrier = pltpu.get_barrier_semaphore()
    for step in order:
        to = {"mode": partner(me, step)}
        pl.semaphore_signal(barrier, inc=1, device_id=to, device_id_type=pl.DeviceIdType.MESH)
    if sides > 1:
        pl.semaphore_signal(barrier, inc=1, device_id=other, device_id_type=pl.DeviceIdType.MESH)

    local(coef_ref, coef_in, own_sems.at[0]).wait()
    early = [local(a, b, own_sems.at[4 + i]) for i, (a, b) in enumerate(zip(table_refs, tables))]
    coef_own[...] = pack_coef(swap_rows(coef_in[...]))
    pl.semaphore_wait(barrier, parts - 1 + (sides > 1))

    slot = iter(range(sends.shape[0]))
    column, row_of = me % plane, me // plane

    def send_all(here, there, steps_of=order):
        at = next(slot)
        return [
            remote(here(partner(me, step)), there, sends.at[at, step], recvs.at[at, step],
                   {"mode": partner(me, step)})
            for step in steps_of
        ]

    own_coef = coefs.at[column, row_of]
    first = send_all(lambda to: coef_own, own_coef, [step for step in order if step % plane == 0])
    first.append(local(coef_own, own_coef, own_sems.at[0]))
    listed = send_all(lambda to: list_ref, lists.at[me])
    listed.append(local(list_ref, lists.at[me], own_sems.at[1]))

    def chunk(to, part):
        at = pl.multiple_of(to * steps + part * half, FT)
        return x_ref.at[:, :, pl.ds(at, half)]

    def send_field(part):
        copies = send_all(lambda to: chunk(to, part), timed.at[part, me])
        copies.append(local(chunk(me, part), timed.at[part, me], own_sems.at[10 + part]))
        return copies

    field_copies = [send_field(0)]
    for copy in first:
        copy.wait()
    second = send_all(lambda to: coefs.at[column], coefs.at[column],
                      [step for step in order if step < plane])
    field_copies += [send_field(part) for part in range(1, pieces)]
    for copy in listed:
        copy.wait()
    local(lists, list_s, own_sems.at[2]).wait()
    blocks = lists.shape[0]
    owners = owner_table(blocks, width, list_s)
    for copy in second:
        copy.wait()

    mode_copies = [[] for _ in range(halves)]
    mode_slot = {}

    def send_stepped(part, h):
        copies = send_all(lambda to: stepped.at[part, h, to], by_mode.at[part, h, me])
        copies.append(
            local(stepped.at[part, h, me], by_mode.at[part, h, me], own_sems.at[20 + part * halves + h])
        )
        mode_copies[h].append((part, copies))

    early_parts = max(pieces - 2, 0)
    for part, copies in enumerate(field_copies):
        for copy in copies:
            copy.wait()
        for c in range(2):
            fld[c] = timed[part, :, c].astype(jnp.float32).reshape(groups, MB, half)

        def one_block(k, carry):
            kerr_terms_of(k, list_s, unpack_coef(coefs[k % plane, k // plane]), fld, terms)
            return carry

        lax.fori_loop(0, blocks, one_block, 0, unroll=2)
        for c in range(2):
            term = terms[1 - c]
            high = term.astype(HALF)
            low = (term - high.astype(jnp.float32)).astype(HALF)
            kerr = jnp.dot(owners, high, preferred_element_type=jnp.float32)
            kerr = kerr + jnp.dot(owners, low, preferred_element_type=jnp.float32)
            turn = kerr_strength * (2 * c - 1)
            new = fld[c].reshape(width, half) + turn * kerr
            new = new.reshape(parts, halves, SUB, half)
            for h in range(halves):
                stack = [new[:, h, :, n * FT : (n + 1) * FT] for n in range(tiles)]
                stepped[part, h, :, c] = jnp.concatenate(stack, axis=1).astype(HALF)
        if part < early_parts:
            for h in range(halves):
                send_stepped(part, h)
    for h in range(halves):
        for part in range(early_parts, pieces):
            send_stepped(part, h)
    for copy in early:
        copy.wait()

    def send_spectra(h):
        copies = send_all(lambda to: spec.at[h, to], out_ref.at[0, h, me])
        own = local(spec.at[h, me], out_ref.at[0, h, me], own_sems.at[3 if h else 0])
        passed = []
        if sides > 1:
            at = next(slot)
            passed.append(remote(spec.at[h, me], out_ref.at[1, h, me], sends.at[at, 0], recvs.at[at, 0], other))
        else:
            at = None
        return copies, own, passed, at

    outgoing = []
    for h in range(halves):
        for part, copies in mode_copies[h]:
            for copy in copies:
                copy.wait()
            for c in range(2):
                for n in range(tiles):
                    xf[c, :, part * tiles + n] = by_mode[
                        part, h, :, c, n * SUB : (n + 1) * SUB
                    ].astype(jnp.float32)
        dft_modes(xf, rows, tables)
        spec[h] = rows[...].reshape(spec.shape[1:]).astype(HALF)
        outgoing.append(send_spectra(h))
    for h, (copies, own, passed, at) in enumerate(outgoing):
        for step, copy in zip(order, copies):
            copy.wait_recv()
            if sides > 1:
                source = partner(me, step)
                passed.append(
                    remote(out_ref.at[0, h, source], out_ref.at[1, h, source],
                           sends.at[at, step], recvs.at[at, step], other)
                )
    for copies, own, passed, _ in outgoing:
        own.wait()
        for copy in copies:
            copy.wait_send()
        for copy in passed:
            copy.wait()


def spectra_of(field, coef, listed, parts, sides):
    _, modes, times = field.shape
    steps = times // parts
    width = parts * modes
    fine = steps // FT
    halves = modes // SUB
    pieces = max(fine // 2, 1)
    half = steps // pieces
    tiles = half // FT
    plane = plane_size(parts)
    tables = dft_tables()
    slots = 3 + pieces * (1 + halves) + 2 * halves
    packed = (coef.shape[0] // 2, coef.shape[1] * 2)
    spread = (halves, parts, fine, 2 * SUB, FT)
    return pl.pallas_call(
        functools.partial(whole_kernel, parts, sides, pieces),
        out_shape=jax.ShapeDtypeStruct((sides,) + spread, HALF),
        in_specs=[pl.BlockSpec(memory_space=pltpu.HBM)] * (3 + len(tables)),
        out_specs=pl.BlockSpec(memory_space=ANY),
        scratch_shapes=[
            VMEM((pieces, parts, 2, modes, half), HALF),
            VMEM(coef.shape, HALF),
            VMEM(packed, HALF),
            VMEM((plane, parts // plane) + packed, HALF),
            VMEM((parts,) + listed.shape, jnp.int32),
            pltpu.SMEM((parts,) + listed.shape, jnp.int32),
            VMEM((2, width // MB, MB, half), jnp.float32),
            VMEM((2, parts * MB, half), jnp.float32),
            VMEM((pieces, halves, parts, 2, tiles * SUB, FT), HALF),
            VMEM((pieces, halves, parts, 2, tiles * SUB, FT), HALF),
            VMEM((2, parts, fine, SUB, FT), jnp.float32),
            VMEM((2 * FT * SUB, FT), jnp.float32),
            VMEM(spread, HALF),
        ]
        + [VMEM(t.shape, t.dtype) for t in tables]
        + [
            pltpu.SemaphoreType.DMA((slots, parts)),
            pltpu.SemaphoreType.DMA((slots, parts)),
            pltpu.SemaphoreType.DMA((20 + pieces * halves,)),
        ],
        compiler_params=pltpu.CompilerParams(
            collective_id=0, has_side_effects=True, vmem_limit_bytes=28 * 1024 * 1024
        ),
    )(*(pltpu.with_memory_space_constraint(a, pltpu.HBM) for a in (field, coef, listed, *tables)))


def dft_tables():
    a = np.arange(FT)
    four = np.exp(-2j * np.pi / FT * (np.outer(a, a) % FT))
    twist = np.exp(-2j * np.pi / NT * (np.outer(a, a) % NT)) / FT
    first = np.block([[four.real, -four.imag], [four.imag, four.real]])
    second = first.reshape(2, FT, 2 * FT).transpose(1, 0, 2).reshape(2 * FT, 2 * FT)

    def split(t):
        t = t.astype(np.float32)
        high = t.astype(HALF)
        return high, (t - high.astype(np.float32)).astype(HALF)

    return (
        *split(first),
        twist.real.astype(np.float32),
        twist.imag.astype(np.float32),
        *split(second),
    )


def dft_modes(xf, rows, tables):
    f1h, f1l, tw_re, tw_im, f2h, f2l = tables
    flat = xf.reshape(2 * FT * SUB, FT)
    nt = (((1,), (1,)), ((), ()))
    dot = functools.partial(jnp.dot, preferred_element_type=jnp.float32)
    dot_nt = functools.partial(
        lax.dot_general, dimension_numbers=nt, preferred_element_type=jnp.float32
    )
    for m in range(0, SUB, 2):
        x = jnp.concatenate(
            [flat[pl.ds(m + i, 2 * FT, stride=SUB), :].astype(HALF) for i in range(2)], axis=1
        )
        half = dot(f1h[...], x) + dot(f1l[...], x)
        turned = []
        for i in range(2):
            h_re, h_im = half[:FT, i * FT : (i + 1) * FT], half[FT:, i * FT : (i + 1) * FT]
            turned.append(
                jnp.concatenate(
                    [
                        h_re * tw_re[...] - h_im * tw_im[...],
                        h_re * tw_im[...] + h_im * tw_re[...],
                    ],
                    axis=1,
                )
            )
        turned = jnp.concatenate(turned, axis=0)
        high = turned.astype(HALF)
        low = (turned - high.astype(jnp.float32)).astype(HALF)
        out = dot_nt(f2h[...], high) + dot_nt(f2h[...], low) + dot_nt(f2l[...], high)
        for i in range(2):
            rows[pl.ds(m + i, 2 * FT, stride=SUB), :] = out[:, i * FT : (i + 1) * FT]


def gram_kernel(scale, spec_ref, out_ref, held, sems):
    sides, halves, parts, high, _, _ = spec_ref.shape
    _, per, _, row_count, width = held.shape
    sources = row_count // (halves * SUB)
    first = lax.axis_index("real") * sources
    lane = lax.broadcasted_iota(jnp.int32, (2 * row_count, 2 * sides * FT), 1)
    band = (lane % FT) // FB

    def gathered(side, j, at, count):
        parts_of = [
            spec_ref[side, h, at, j].astype(jnp.float32).reshape(count, 2, SUB, FT)
            for h in range(halves)
        ]
        return [
            jnp.stack([p[:, c] for p in parts_of], axis=1).reshape(count * halves * SUB, FT).astype(HALF)
            for c in range(2)
        ]

    def out_copy(j):
        return pltpu.make_async_copy(held.at[j], out_ref.at[pl.ds(j * per, per)], sems.at[j])

    def one_high(j, carry):
        cols, rows_re, rows_im = [], [], []
        for side in range(sides):
            re, im = gathered(side, j, pl.ds(0, parts), parts)
            own_re, own_im = gathered(side, j, pl.ds(first, sources), sources)
            cols += [re, im]
            rows_re += [own_re, own_im]
            rows_im += [own_im, -own_re]
        cols = jnp.concatenate(cols, axis=1)
        rows = jnp.concatenate(
            [jnp.concatenate(rows_re, axis=1), jnp.concatenate(rows_im, axis=1)], axis=0
        )
        for g in range(per):
            kept = jnp.where(band == g, rows, jnp.zeros_like(rows))
            out = lax.dot_general(
                kept, cols, (((1,), (1,)), ((), ())), preferred_element_type=jnp.float32
            )
            held[j, g] = (out * scale).reshape(2, row_count, width)
        out_copy(j).start()
        return carry

    lax.fori_loop(0, high, one_high, 0)
    for j in range(high):
        out_copy(j).wait()


def gram(spectra, row_count, scale):
    sides, halves, parts, high, _, _ = spectra.shape
    width = parts * halves * SUB
    per = FT // FB
    shape = (per, 2, row_count, width)
    return pl.pallas_call(
        functools.partial(gram_kernel, scale),
        out_shape=jax.ShapeDtypeStruct((high * per,) + shape[1:], jnp.float32),
        in_specs=[pl.BlockSpec(memory_space=VMEM)],
        out_specs=pl.BlockSpec(memory_space=ANY),
        scratch_shapes=[VMEM((high,) + shape, jnp.float32), pltpu.SemaphoreType.DMA((high,))],
        compiler_params=pltpu.CompilerParams(vmem_limit_bytes=24 * 1024 * 1024),
    )(spectra)


def tiled_shards(input_field, kerr_coeff, block_list):
    parts, sides = lax.axis_size("mode"), lax.axis_size("real")
    _, _, modes, times = input_field.shape
    width = parts * modes
    spectra = spectra_of(
        input_field.reshape(2, modes, times), kerr_coeff[0], block_list, parts, sides
    )
    return gram(spectra, width // sides, 1.0 / (FB * sides))


def tiles_fit(mesh):
    parts = mesh.shape["mode"]
    return FT % parts == 0 and (2 * FT // parts) % 16 == 0 and mesh.shape["real"] <= 2


def either(mesh, input_field, kerr_coeff, block_list):
    modes = input_field.shape[2]
    blocks_each = kerr_coeff.shape[0]
    fits = tiles_fit(mesh) and modes % 16 == 0 and blocks_each == 1
    fits = fits and input_field.shape[1] == 1 and input_field.shape[3] == NT
    return (tiled_shards if fits else shards)(input_field, kerr_coeff, block_list)


def solution(mesh):
    return jax.shard_map(
        functools.partial(either, mesh),
        mesh=mesh,
        in_specs=(P(None, "real", "mode", None), P("mode", None, None), P("mode", None)),
        out_specs=P("mode", None, "real", None),
        check_vma=False,
    )
```

time: 101 us -> 89.5 us (0.89)
  Pallas kernels: 101 us -> 89.3 us
    pallas_call x2, Pallas kernels: 101 us -> 89.3 us  [the longest x1 84.4 us: spectra_of(): pl.pallas_call(functools.partial(whole_kernel, parts, sides, pieces), out...]
where the time goes in v1:
time: 89.5 us; the launch traced here: 89.3 us
  Pallas kernels  89.3 us (100%)
    pallas_call x1, Pallas kernels, spectra_of(): pl.pallas_call(functools.partial(whole_kernel, parts, sides, pieces), out...  84.4 us
    pallas_call x1, Pallas kernels, gram(): pl.pallas_call(functools.partial(gram_kernel, scale), out_shape=jax.Shape...  4.89 us

profile of v1, /device:TPU:0, one launch (start us, length us, event | category | flops | bytes accessed | tf_op | source)
XLA Modules:
  0.0 89.3 jit_solution(16125592480255762920)
XLA Ops:
  0.0 84.4 %shard_map.91.spec_ref = bf16[2,2,16,8,16,128]{5,4,3,2,1,0:T(8,128)(2,1)S(1)} custom-call(bf16[2,16,16384]{2,1,0:T(8,128)(2,1)} %bitcast.2, bf16[64,64]{1,0:T(8,128)(2,1)} %bitcast.3, s32[1,4]{1,0:T(1,128)} %list_ref.1, bf16[256,256]{1,0:T(8,128)(2,1)} %constant.12.clone.refs_0_, bf16[256,256]{1,0:T(8,128)(2,1)} %constant.13.clone.refs_1_, ...), custom_call_target="tpu_custom_call" | custom-call | tf_op jit(solution)/shard_map/pallas_call | solution.py:394
  84.4 4.9 %shard_map.92 = f32[32,2,128,256]{3,2,1,0:T(8,128)} custom-call(bf16[2,2,16,8,16,128]{5,4,3,2,1,0:T(8,128)(2,1)S(1)} %shard_map.91.spec_ref), custom_call_target="tpu_custom_call" | custom-call | tf_op jit(solution)/shard_map/pallas_call | solution.py:531

commit v2 on v1

--- a/solution.py
+++ b/solution.py
@@ -148,8 +148,7 @@
 
 
 def partner_order(parts):
-    plane = plane_size(parts)
-    return sorted(range(1, parts), key=lambda step: (-(step // plane), step))
+    return list(range(1, parts))
 
 
 def partner(me, step):
@@ -180,9 +179,9 @@
     return copy
 
 
-def kerr_terms_of(k, list_s, coef, fld, terms):
+def kerr_terms_of(k, at, list_s, coef, fld, terms):
     piece = fld.shape[3]
-    bl, bm, bn = (list_s[k, 0, i] for i in (1, 2, 3))
+    bl, bm, bn = (list_s[*at, 0, i] for i in (1, 2, 3))
     m_re, m_im = fld[0, bm][:, None], fld[1, bm][:, None]
     n_re, n_im = fld[0, bn][None], fld[1, bn][None]
     p_re = (m_re * n_re + m_im * n_im).reshape(MB * MB, piece)
@@ -192,9 +191,9 @@
     w_re = w[:, :piece].reshape(MB, MB, piece)
     w_im = w[:, piece:].reshape(MB, MB, piece)
     l_re, l_im = fld[0, bl][:, None], fld[1, bl][:, None]
-    at = pl.ds(pl.multiple_of(k * MB, MB), MB)
-    terms[0, at] = jnp.sum(w_re * l_re - w_im * l_im, axis=0)
-    terms[1, at] = jnp.sum(w_re * l_im + w_im * l_re, axis=0)
+    row = pl.ds(pl.multiple_of(k * MB, MB), MB)
+    terms[0, row] = jnp.sum(w_re * l_re - w_im * l_im, axis=0)
+    terms[1, row] = jnp.sum(w_re * l_im + w_im * l_re, axis=0)
 
 
 def owner_table(blocks, width, list_s):
@@ -202,8 +201,9 @@
     row = lax.broadcasted_iota(jnp.int32, shape, 0)
     col = lax.broadcasted_iota(jnp.int32, shape, 1)
     wanted = jnp.full(shape, -1, jnp.int32)
+    plane = plane_size(blocks)
     for k in range(blocks):
-        wanted = jnp.where(col // MB == k, list_s[k, 0, 0] * MB + col % MB, wanted)
+        wanted = jnp.where(col // MB == k, list_s[k % plane, k // plane, 0, 0] * MB + col % MB, wanted)
     return (row == wanted).astype(jnp.float32).astype(HALF)
 
 
@@ -267,8 +267,9 @@
     own_coef = coefs.at[column, row_of]
     first = send_all(lambda to: coef_own, own_coef, [step for step in order if step % plane == 0])
     first.append(local(coef_own, own_coef, own_sems.at[0]))
-    listed = send_all(lambda to: list_ref, lists.at[me])
-    listed.append(local(list_ref, lists.at[me], own_sems.at[1]))
+    own_list = lists.at[column, row_of]
+    first += send_all(lambda to: list_ref, own_list, [step for step in order if step % plane == 0])
+    first.append(local(list_ref, own_list, own_sems.at[1]))
 
     def chunk(to, part):
         at = pl.multiple_of(to * steps + part * half, FT)
@@ -282,19 +283,18 @@
     field_copies = [send_field(0)]
     for copy in first:
         copy.wait()
-    second = send_all(lambda to: coefs.at[column], coefs.at[column],
-                      [step for step in order if step < plane])
+    near = [step for step in order if step < plane]
+    listed = send_all(lambda to: lists.at[column], lists.at[column], near)
+    second = send_all(lambda to: coefs.at[column], coefs.at[column], near)
     field_copies += [send_field(part) for part in range(1, pieces)]
     for copy in listed:
         copy.wait()
     local(lists, list_s, own_sems.at[2]).wait()
-    blocks = lists.shape[0]
-    owners = owner_table(blocks, width, list_s)
+    owners = owner_table(parts, width, list_s)
     for copy in second:
         copy.wait()
 
     mode_copies = [[] for _ in range(halves)]
-    mode_slot = {}
 
     def send_stepped(part, h):
         copies = send_all(lambda to: stepped.at[part, h, to], by_mode.at[part, h, me])
@@ -303,7 +303,6 @@
         )
         mode_copies[h].append((part, copies))
 
-    early_parts = max(pieces - 2, 0)
     for part, copies in enumerate(field_copies):
         for copy in copies:
             copy.wait()
@@ -311,10 +310,11 @@
             fld[c] = timed[part, :, c].astype(jnp.float32).reshape(groups, MB, half)
 
         def one_block(k, carry):
-            kerr_terms_of(k, list_s, unpack_coef(coefs[k % plane, k // plane]), fld, terms)
+            at = (k % plane, k // plane)
+            kerr_terms_of(k, at, list_s, unpack_coef(coefs[at]), fld, terms)
             return carry
 
-        lax.fori_loop(0, blocks, one_block, 0, unroll=2)
+        lax.fori_loop(0, parts, one_block, 0, unroll=2)
         for c in range(2):
             term = terms[1 - c]
             high = term.astype(HALF)
@@ -327,11 +327,9 @@
             for h in range(halves):
                 stack = [new[:, h, :, n * FT : (n + 1) * FT] for n in range(tiles)]
                 stepped[part, h, :, c] = jnp.concatenate(stack, axis=1).astype(HALF)
-        if part < early_parts:
-            for h in range(halves):
-                send_stepped(part, h)
-    for h in range(halves):
-        for part in range(early_parts, pieces):
+        send_stepped(part, 0)
+    for h in range(1, halves):
+        for part in range(pieces):
             send_stepped(part, h)
     for copy in early:
         copy.wait()
@@ -358,7 +356,7 @@
                         part, h, :, c, n * SUB : (n + 1) * SUB
                     ].astype(jnp.float32)
         dft_modes(xf, rows, tables)
-        spec[h] = rows[...].reshape(spec.shape[1:]).astype(HALF)
+        spec[h] = pair_lanes(rows[...]).reshape(spec.shape[1:]).astype(HALF)
         outgoing.append(send_spectra(h))
     for h, (copies, own, passed, at) in enumerate(outgoing):
         for step, copy in zip(order, copies):
@@ -388,7 +386,7 @@
     tiles = half // FT
     plane = plane_size(parts)
     tables = dft_tables()
-    slots = 3 + pieces * (1 + halves) + 2 * halves
+    slots = 4 + pieces * (1 + halves) + 2 * halves
     packed = (coef.shape[0] // 2, coef.shape[1] * 2)
     spread = (halves, parts, fine, 2 * SUB, FT)
     return pl.pallas_call(
@@ -401,8 +399,8 @@
             VMEM(coef.shape, HALF),
             VMEM(packed, HALF),
             VMEM((plane, parts // plane) + packed, HALF),
-            VMEM((parts,) + listed.shape, jnp.int32),
-            pltpu.SMEM((parts,) + listed.shape, jnp.int32),
+            VMEM((plane, parts // plane) + listed.shape, jnp.int32),
+            pltpu.SMEM((plane, parts // plane) + listed.shape, jnp.int32),
             VMEM((2, width // MB, MB, half), jnp.float32),
             VMEM((2, parts * MB, half), jnp.float32),
             VMEM((pieces, halves, parts, 2, tiles * SUB, FT), HALF),
@@ -476,13 +474,23 @@
             rows[pl.ds(m + i, 2 * FT, stride=SUB), :] = out[:, i * FT : (i + 1) * FT]
 
 
+def pair_lanes(rows):
+    both = rows.reshape(FT, 2, SUB, FT)
+    re, im = both[:, 0], both[:, 1]
+    left = lax.broadcasted_iota(jnp.int32, re.shape, 2) < FT // 2
+    low = jnp.where(left, re, pltpu.roll(im, FT // 2, 2))
+    high = jnp.where(left, pltpu.roll(re, FT // 2, 2), im)
+    return jnp.stack([low, high], axis=1)
+
+
 def gram_kernel(scale, spec_ref, out_ref, held, sems):
     sides, halves, parts, high, _, _ = spec_ref.shape
     _, per, _, row_count, width = held.shape
     sources = row_count // (halves * SUB)
     first = lax.axis_index("real") * sources
-    lane = lax.broadcasted_iota(jnp.int32, (2 * row_count, 2 * sides * FT), 1)
-    band = (lane % FT) // FB
+    each = per // 2
+    lane = lax.broadcasted_iota(jnp.int32, (2 * row_count, sides * FT), 1)
+    band = lane % (FT // 2) // FB
 
     def gathered(side, j, at, count):
         parts_of = [
@@ -490,31 +498,36 @@
             for h in range(halves)
         ]
         return [
-            jnp.stack([p[:, c] for p in parts_of], axis=1).reshape(count * halves * SUB, FT).astype(HALF)
-            for c in range(2)
+            jnp.stack([p[:, i] for p in parts_of], axis=1).reshape(count * halves * SUB, FT)
+            for i in range(2)
         ]
+
+    def turned(x):
+        moved = pltpu.roll(x, FT // 2, 1)
+        at = lax.broadcasted_iota(jnp.int32, x.shape, 1)
+        return jnp.where(at < FT // 2, moved, -moved)
 
     def out_copy(j):
         return pltpu.make_async_copy(held.at[j], out_ref.at[pl.ds(j * per, per)], sems.at[j])
 
     def one_high(j, carry):
-        cols, rows_re, rows_im = [], [], []
-        for side in range(sides):
-            re, im = gathered(side, j, pl.ds(0, parts), parts)
-            own_re, own_im = gathered(side, j, pl.ds(first, sources), sources)
-            cols += [re, im]
-            rows_re += [own_re, own_im]
-            rows_im += [own_im, -own_re]
-        cols = jnp.concatenate(cols, axis=1)
-        rows = jnp.concatenate(
-            [jnp.concatenate(rows_re, axis=1), jnp.concatenate(rows_im, axis=1)], axis=0
-        )
-        for g in range(per):
-            kept = jnp.where(band == g, rows, jnp.zeros_like(rows))
-            out = lax.dot_general(
-                kept, cols, (((1,), (1,)), ((), ())), preferred_element_type=jnp.float32
-            )
-            held[j, g] = (out * scale).reshape(2, row_count, width)
+        cols = [gathered(side, j, pl.ds(0, parts), parts) for side in range(sides)]
+        own = [gathered(side, j, pl.ds(first, sources), sources) for side in range(sides)]
+        for i in range(2):
+            col = jnp.concatenate([c[i] for c in cols], axis=1).astype(HALF)
+            row = jnp.concatenate(
+                [
+                    jnp.concatenate([o[i] for o in own], axis=1),
+                    jnp.concatenate([turned(o[i]) for o in own], axis=1),
+                ],
+                axis=0,
+            ).astype(HALF)
+            for g in range(each):
+                kept = jnp.where(band == g, row, jnp.zeros_like(row))
+                out = lax.dot_general(
+                    kept, col, (((1,), (1,)), ((), ())), preferred_element_type=jnp.float32
+                )
+                held[j, i * each + g] = (out * scale).reshape(2, row_count, width)
         out_copy(j).start()
         return carry
 

time: 89.5 us -> 85.9 us (0.960)
  Pallas kernels: 89.3 us -> 85.7 us
    pallas_call x1, Pallas kernels: 84.4 us -> 81.8 us  [spectra_of(): pl.pallas_call(functools.partial(whole_kernel, parts, sides, pieces), out...]
    pallas_call x1, Pallas kernels: 4.89 us -> 3.86 us  [gram(): pl.pallas_call(functools.partial(gram_kernel, scale), out_shape=jax.Shape...]
where the time goes in v2:
time: 85.9 us; the launch traced here: 85.7 us
  Pallas kernels  85.7 us (100%)
    pallas_call x1, Pallas kernels, spectra_of(): pl.pallas_call(functools.partial(whole_kernel, parts, sides, pieces), out...  81.8 us
    pallas_call x1, Pallas kernels, gram(): pl.pallas_call(functools.partial(gram_kernel, scale), out_shape=jax.Shape...  3.86 us

profile of v2, /device:TPU:0, one launch (start us, length us, event | category | flops | bytes accessed | tf_op | source)
XLA Modules:
  0.0 85.7 jit_solution(4903918806880730117)
XLA Ops:
  0.0 81.8 %shard_map.91.spec_ref = bf16[2,2,16,8,16,128]{5,4,3,2,1,0:T(8,128)(2,1)S(1)} custom-call(bf16[2,16,16384]{2,1,0:T(8,128)(2,1)} %bitcast.2, bf16[64,64]{1,0:T(8,128)(2,1)} %bitcast.3, s32[1,4]{1,0:T(1,128)} %list_ref.1, bf16[256,256]{1,0:T(8,128)(2,1)} %constant.12.clone.refs_0_, bf16[256,256]{1,0:T(8,128)(2,1)} %constant.13.clone.refs_1_, ...), custom_call_target="tpu_custom_call" | custom-call | tf_op jit(solution)/shard_map/pallas_call | solution.py:392
  81.8 3.9 %shard_map.92 = f32[32,2,128,256]{3,2,1,0:T(8,128)} custom-call(bf16[2,2,16,8,16,128]{5,4,3,2,1,0:T(8,128)(2,1)S(1)} %shard_map.91.spec_ref), custom_call_target="tpu_custom_call" | custom-call | tf_op jit(solution)/shard_map/pallas_call | solution.py:544

commit v3 on v2

--- a/solution.py
+++ b/solution.py
@@ -179,21 +179,21 @@
     return copy
 
 
-def kerr_terms_of(k, at, list_s, coef, fld, terms):
-    piece = fld.shape[3]
+def kerr_terms_of(k, at, piece, list_s, coef, fld, terms):
+    span = pl.ds(0, piece)
     bl, bm, bn = (list_s[*at, 0, i] for i in (1, 2, 3))
-    m_re, m_im = fld[0, bm][:, None], fld[1, bm][:, None]
-    n_re, n_im = fld[0, bn][None], fld[1, bn][None]
+    m_re, m_im = fld[0, bm, :, span][:, None], fld[1, bm, :, span][:, None]
+    n_re, n_im = fld[0, bn, :, span][None], fld[1, bn, :, span][None]
     p_re = (m_re * n_re + m_im * n_im).reshape(MB * MB, piece)
     p_im = (m_im * n_re - m_re * n_im).reshape(MB * MB, piece)
     pairs = jnp.concatenate([p_re, p_im], axis=1).astype(HALF)
     w = jnp.dot(coef, pairs, preferred_element_type=jnp.float32)
     w_re = w[:, :piece].reshape(MB, MB, piece)
     w_im = w[:, piece:].reshape(MB, MB, piece)
-    l_re, l_im = fld[0, bl][:, None], fld[1, bl][:, None]
+    l_re, l_im = fld[0, bl, :, span][:, None], fld[1, bl, :, span][:, None]
     row = pl.ds(pl.multiple_of(k * MB, MB), MB)
-    terms[0, row] = jnp.sum(w_re * l_re - w_im * l_im, axis=0)
-    terms[1, row] = jnp.sum(w_re * l_im + w_im * l_re, axis=0)
+    terms[0, row, span] = jnp.sum(w_re * l_re - w_im * l_im, axis=0)
+    terms[1, row, span] = jnp.sum(w_re * l_im + w_im * l_re, axis=0)
 
 
 def owner_table(blocks, width, list_s):
@@ -220,12 +220,13 @@
     return jnp.concatenate([coef[:rows], coef[rows:]], axis=1)
 
 
-def unpack_coef(packed):
+def unpack_coef(pieces):
+    packed = jnp.concatenate(pieces, axis=0)
     lanes = packed.shape[1] // 2
     return jnp.concatenate([packed[:, :lanes], packed[:, lanes:]], axis=0)
 
 
-def whole_kernel(parts, sides, pieces, x_ref, coef_ref, list_ref, *refs):
+def whole_kernel(parts, sides, cuts, x_ref, coef_ref, list_ref, *refs):
     table_refs, out_ref = refs[:6], refs[6]
     (timed, coef_in, coef_own, coefs, lists, list_s, fld, terms, stepped, by_mode, xf, rows, spec) = refs[7:20]
     tables, (sends, recvs, own_sems) = refs[20:26], refs[26:]
@@ -235,9 +236,9 @@
     steps = times // parts
     width = parts * modes
     groups = width // MB
-    half = steps // pieces
-    tiles = half // FT
     fine = steps // FT
+    pieces = len(cuts)
+    starts = [sum(cuts[:part]) for part in range(pieces)]
     halves = modes // SUB
     order = partner_order(parts)
     plane = plane_size(parts)
@@ -250,7 +251,7 @@
 
     local(coef_ref, coef_in, own_sems.at[0]).wait()
     early = [local(a, b, own_sems.at[4 + i]) for i, (a, b) in enumerate(zip(table_refs, tables))]
-    coef_own[...] = pack_coef(swap_rows(coef_in[...]))
+    coef_own[...] = pack_coef(swap_rows(coef_in[...])).reshape(coef_own.shape)
     pl.semaphore_wait(barrier, parts - 1 + (sides > 1))
 
     slot = iter(range(sends.shape[0]))
@@ -264,20 +265,25 @@
             for step in steps_of
         ]
 
-    own_coef = coefs.at[column, row_of]
-    first = send_all(lambda to: coef_own, own_coef, [step for step in order if step % plane == 0])
-    first.append(local(coef_own, own_coef, own_sems.at[0]))
+    side = lax.axis_index("real")
+    own_coef = coefs.at[side, column, row_of]
+    mine = coef_own.at[side]
+    first = send_all(lambda to: mine, own_coef, [step for step in order if step % plane == 0])
+    first.append(local(mine, own_coef, own_sems.at[0]))
     own_list = lists.at[column, row_of]
     first += send_all(lambda to: list_ref, own_list, [step for step in order if step % plane == 0])
     first.append(local(list_ref, own_list, own_sems.at[1]))
 
     def chunk(to, part):
-        at = pl.multiple_of(to * steps + part * half, FT)
-        return x_ref.at[:, :, pl.ds(at, half)]
+        at = pl.multiple_of(to * steps + starts[part] * FT, FT)
+        return x_ref.at[:, :, pl.ds(at, cuts[part] * FT)]
+
+    def landing(part):
+        return timed.at[me, :, :, pl.ds(starts[part] * FT, cuts[part] * FT)]
 
     def send_field(part):
-        copies = send_all(lambda to: chunk(to, part), timed.at[part, me])
-        copies.append(local(chunk(me, part), timed.at[part, me], own_sems.at[10 + part]))
+        copies = send_all(lambda to: chunk(to, part), landing(part))
+        copies.append(local(chunk(me, part), landing(part), own_sems.at[10 + part]))
         return copies
 
     field_copies = [send_field(0)]
@@ -285,7 +291,7 @@
         copy.wait()
     near = [step for step in order if step < plane]
     listed = send_all(lambda to: lists.at[column], lists.at[column], near)
-    second = send_all(lambda to: coefs.at[column], coefs.at[column], near)
+    second = send_all(lambda to: coefs.at[side, column], coefs.at[side, column], near)
     field_copies += [send_field(part) for part in range(1, pieces)]
     for copy in listed:
         copy.wait()
@@ -293,49 +299,85 @@
     owners = owner_table(parts, width, list_s)
     for copy in second:
         copy.wait()
+    if sides > 1:
+        at = next(slot)
+        remote(coefs.at[side], coefs.at[side], sends.at[at, 0], recvs.at[at, 0], other).wait()
 
     mode_copies = [[] for _ in range(halves)]
 
-    def send_stepped(part, h):
-        copies = send_all(lambda to: stepped.at[part, h, to], by_mode.at[part, h, me])
-        copies.append(
-            local(stepped.at[part, h, me], by_mode.at[part, h, me], own_sems.at[20 + part * halves + h])
-        )
-        mode_copies[h].append((part, copies))
+    def send_stepped(h, first_tile, tiles):
+        some = pl.ds(first_tile // 2, tiles // 2)
+        copies = send_all(lambda to: stepped.at[h, to, some], by_mode.at[h, me, some])
+        at = own_sems.at[20 + halves * pieces + h if tiles == fine else 20 + h * pieces + starts.index(first_tile)]
+        copies.append(local(stepped.at[h, me, some], by_mode.at[h, me, some], at))
+        mode_copies[h].append((first_tile, tiles, copies))
 
     for part, copies in enumerate(field_copies):
         for copy in copies:
             copy.wait()
+        tiles = cuts[part]
+        half = tiles * FT
+        here, span = pl.ds(0, half), pl.ds(starts[part] * FT, half)
         for c in range(2):
-            fld[c] = timed[part, :, c].astype(jnp.float32).reshape(groups, MB, half)
+            fld[c, :, :, here] = timed[:, c, :, span].astype(jnp.float32).reshape(groups, MB, half)
 
         def one_block(k, carry):
             at = (k % plane, k // plane)
-            kerr_terms_of(k, at, list_s, unpack_coef(coefs[at]), fld, terms)
+            coef = unpack_coef([coefs[i, *at] for i in range(sides)])
+            kerr_terms_of(k, at, half, list_s, coef, fld, terms)
             return carry
 
         lax.fori_loop(0, parts, one_block, 0, unroll=2)
         for c in range(2):
-            term = terms[1 - c]
+            term = terms[1 - c, :, here]
             high = term.astype(HALF)
             low = (term - high.astype(jnp.float32)).astype(HALF)
             kerr = jnp.dot(owners, high, preferred_element_type=jnp.float32)
             kerr = kerr + jnp.dot(owners, low, preferred_element_type=jnp.float32)
             turn = kerr_strength * (2 * c - 1)
-            new = fld[c].reshape(width, half) + turn * kerr
+            new = fld[c, :, :, here].reshape(width, half) + turn * kerr
             new = new.reshape(parts, halves, SUB, half)
             for h in range(halves):
-                stack = [new[:, h, :, n * FT : (n + 1) * FT] for n in range(tiles)]
-                stepped[part, h, :, c] = jnp.concatenate(stack, axis=1).astype(HALF)
-        send_stepped(part, 0)
+                for n in range(0, tiles, 2):
+                    pair = [new[:, h, :, (n + i) * FT : (n + i + 1) * FT] for i in range(2)]
+                    stepped[h, :, (starts[part] + n) // 2, c] = jnp.concatenate(pair, axis=1).astype(HALF)
+        send_stepped(0, starts[part], tiles)
     for h in range(1, halves):
-        for part in range(pieces):
-            send_stepped(part, h)
+        send_stepped(h, 0, fine)
     for copy in early:
         copy.wait()
 
+    def is_zero(number):
+        return (parts - number) // parts
+
+    def first_device_first():
+        pairs = []
+        for step in order:
+            if step == order[0]:
+                other_way = is_zero(me)
+                pairs.append((other_way, me + other_way))
+            else:
+                same = is_zero((me - step + parts) % parts)
+                pairs.append(
+                    (
+                        partner(me, step) * (1 - same) + partner(me, order[0]) * same,
+                        step * (1 - same) + order[0] * same,
+                    )
+                )
+        return pairs
+
+
     def send_spectra(h):
-        copies = send_all(lambda to: spec.at[h, to], out_ref.at[0, h, me])
+        listed_targets = first_device_first()
+        at = next(slot)
+        copies = [
+            (
+                remote(spec.at[h, to], out_ref.at[0, h, me], sends.at[at, step], recvs.at[at, step], {"mode": to}),
+                to,
+                step,
+            )
+            for to, step in listed_targets
+        ]
         own = local(spec.at[h, me], out_ref.at[0, h, me], own_sems.at[3 if h else 0])
         passed = []
         if sides > 1:
@@ -347,29 +389,27 @@
 
     outgoing = []
     for h in range(halves):
-        for part, copies in mode_copies[h]:
+        for first_tile, tiles, copies in mode_copies[h]:
             for copy in copies:
                 copy.wait()
-            for c in range(2):
-                for n in range(tiles):
-                    xf[c, :, part * tiles + n] = by_mode[
-                        part, h, :, c, n * SUB : (n + 1) * SUB
-                    ].astype(jnp.float32)
+            for n in range(first_tile, first_tile + tiles, 2):
+                for c in range(2):
+                    pair = by_mode[h, :, n // 2, c].astype(jnp.float32)
+                    xf[c, :, n : n + 2] = pair.reshape(parts, 2, SUB, FT)
         dft_modes(xf, rows, tables)
         spec[h] = pair_lanes(rows[...]).reshape(spec.shape[1:]).astype(HALF)
         outgoing.append(send_spectra(h))
     for h, (copies, own, passed, at) in enumerate(outgoing):
-        for step, copy in zip(order, copies):
+        for copy, source, step in copies:
             copy.wait_recv()
             if sides > 1:
-                source = partner(me, step)
                 passed.append(
                     remote(out_ref.at[0, h, source], out_ref.at[1, h, source],
                            sends.at[at, step], recvs.at[at, step], other)
                 )
     for copies, own, passed, _ in outgoing:
         own.wait()
-        for copy in copies:
+        for copy, _, _ in copies:
             copy.wait_send()
         for copy in passed:
             copy.wait()
@@ -381,30 +421,30 @@
     width = parts * modes
     fine = steps // FT
     halves = modes // SUB
-    pieces = max(fine // 2, 1)
-    half = steps // pieces
-    tiles = half // FT
+    cuts = [fine // 2, fine // 2]
+    pieces = len(cuts)
+    half = max(cuts) * FT
     plane = plane_size(parts)
     tables = dft_tables()
-    slots = 4 + pieces * (1 + halves) + 2 * halves
-    packed = (coef.shape[0] // 2, coef.shape[1] * 2)
+    slots = 5 + pieces * 2 + 3 * halves
+    packed = (coef.shape[0] // 2 // sides, coef.shape[1] * 2)
     spread = (halves, parts, fine, 2 * SUB, FT)
     return pl.pallas_call(
-        functools.partial(whole_kernel, parts, sides, pieces),
+        functools.partial(whole_kernel, parts, sides, cuts),
         out_shape=jax.ShapeDtypeStruct((sides,) + spread, HALF),
         in_specs=[pl.BlockSpec(memory_space=pltpu.HBM)] * (3 + len(tables)),
         out_specs=pl.BlockSpec(memory_space=ANY),
         scratch_shapes=[
-            VMEM((pieces, parts, 2, modes, half), HALF),
+            VMEM((parts, 2, modes, steps), HALF),
             VMEM(coef.shape, HALF),
-            VMEM(packed, HALF),
-            VMEM((plane, parts // plane) + packed, HALF),
+            VMEM((sides,) + packed, HALF),
+            VMEM((sides, plane, parts // plane) + packed, HALF),
             VMEM((plane, parts // plane) + listed.shape, jnp.int32),
             pltpu.SMEM((plane, parts // plane) + listed.shape, jnp.int32),
             VMEM((2, width // MB, MB, half), jnp.float32),
             VMEM((2, parts * MB, half), jnp.float32),
-            VMEM((pieces, halves, parts, 2, tiles * SUB, FT), HALF),
-            VMEM((pieces, halves, parts, 2, tiles * SUB, FT), HALF),
+            VMEM((halves, parts, fine // 2, 2, 2 * SUB, FT), HALF),
+            VMEM((halves, parts, fine // 2, 2, 2 * SUB, FT), HALF),
             VMEM((2, parts, fine, SUB, FT), jnp.float32),
             VMEM((2 * FT * SUB, FT), jnp.float32),
             VMEM(spread, HALF),
@@ -413,7 +453,7 @@
         + [
             pltpu.SemaphoreType.DMA((slots, parts)),
             pltpu.SemaphoreType.DMA((slots, parts)),
-            pltpu.SemaphoreType.DMA((20 + pieces * halves,)),
+            pltpu.SemaphoreType.DMA((20 + (pieces + 1) * halves,)),
         ],
         compiler_params=pltpu.CompilerParams(
             collective_id=0, has_side_effects=True, vmem_limit_bytes=28 * 1024 * 1024

time: 85.9 us -> 84.9 us (0.988)
  the two profiles are of different devices: /device:TPU:0 before, /device:TPU:9 now
where the time goes in v3:
time: 84.9 us; the launch traced here: 84.6 us
  Pallas kernels  84.6 us (100%)
    pallas_call x1, Pallas kernels, spectra_of(): pl.pallas_call(functools.partial(whole_kernel, parts, sides, cuts), out_s...  80.8 us
    pallas_call x1, Pallas kernels, gram(): pl.pallas_call(functools.partial(gram_kernel, scale), out_shape=jax.Shape...  3.87 us

profile of v3, /device:TPU:9, one launch (start us, length us, event | category | flops | bytes accessed | tf_op | source)
XLA Modules:
  0.0 84.6 jit_solution(392517819530360965)
XLA Ops:
  0.0 80.8 %shard_map.91.spec_ref = bf16[2,2,16,8,16,128]{5,4,3,2,1,0:T(8,128)(2,1)S(1)} custom-call(bf16[2,16,16384]{2,1,0:T(8,128)(2,1)} %bitcast.2, bf16[64,64]{1,0:T(8,128)(2,1)} %bitcast.3, s32[1,4]{1,0:T(1,128)} %list_ref.1, bf16[256,256]{1,0:T(8,128)(2,1)} %constant.12.clone.refs_0_, bf16[256,256]{1,0:T(8,128)(2,1)} %constant.13.clone.refs_1_, ...), custom_call_target="tpu_custom_call" | custom-call | tf_op jit(solution)/shard_map/pallas_call | solution.py:432
  80.8 3.9 %shard_map.92 = f32[32,2,128,256]{3,2,1,0:T(8,128)} custom-call(bf16[2,2,16,8,16,128]{5,4,3,2,1,0:T(8,128)(2,1)S(1)} %shard_map.91.spec_ref), custom_call_target="tpu_custom_call" | custom-call | tf_op jit(solution)/shard_map/pallas_call | solution.py:584

commit v4 on v3

--- a/solution.py
+++ b/solution.py
@@ -243,7 +243,7 @@
     order = partner_order(parts)
     plane = plane_size(parts)
     barrier = pltpu.get_barrier_semaphore()
-    for step in order:
+    for step in reversed(order):
         to = {"mode": partner(me, step)}
         pl.semaphore_signal(barrier, inc=1, device_id=to, device_id_type=pl.DeviceIdType.MESH)
     if sides > 1:
@@ -347,45 +347,48 @@
     for copy in early:
         copy.wait()
 
-    def is_zero(number):
-        return (parts - number) // parts
-
-    def first_device_first():
+    def columns_ascending():
         pairs = []
-        for step in order:
-            if step == order[0]:
-                other_way = is_zero(me)
-                pairs.append((other_way, me + other_way))
-            else:
-                same = is_zero((me - step + parts) % parts)
-                pairs.append(
-                    (
-                        partner(me, step) * (1 - same) + partner(me, order[0]) * same,
-                        step * (1 - same) + order[0] * same,
-                    )
-                )
+        for i in range(plane - 1):
+            to = i + (i - column + plane) // plane
+            step, bit = 0, 1
+            while bit < plane:
+                step = step + (to // bit + column // bit) % 2 * bit
+                bit *= 2
+            pairs.append((row_of * plane + to, step))
+        for r in range(1, parts // plane):
+            for k in range(plane):
+                row = partner(me, r * plane) // plane
+                pairs.append((row * plane + k, r * plane + partner(column, k)))
         return pairs
 
+    targets = columns_ascending()
 
     def send_spectra(h):
-        listed_targets = first_device_first()
         at = next(slot)
         copies = [
-            (
-                remote(spec.at[h, to], out_ref.at[0, h, me], sends.at[at, step], recvs.at[at, step], {"mode": to}),
-                to,
-                step,
-            )
-            for to, step in listed_targets
+            remote(spec.at[h, to], out_ref.at[0, h, me], sends.at[at, step], recvs.at[at, step], {"mode": to})
+            for to, step in targets
         ]
         own = local(spec.at[h, me], out_ref.at[0, h, me], own_sems.at[3 if h else 0])
-        passed = []
-        if sides > 1:
-            at = next(slot)
-            passed.append(remote(spec.at[h, me], out_ref.at[1, h, me], sends.at[at, 0], recvs.at[at, 0], other))
-        else:
-            at = None
-        return copies, own, passed, at
+        return copies, own, at
+
+    def arrived(h, at, step):
+        source = partner(me, step)
+        pltpu.make_async_remote_copy(
+            src_ref=spec.at[h, source],
+            dst_ref=out_ref.at[0, h, source],
+            send_sem=sends.at[at, step],
+            recv_sem=recvs.at[at, step],
+            device_id={"mode": source},
+            device_id_type=pl.DeviceIdType.MESH,
+        ).wait_recv()
+
+    def passing(h, some, at, which):
+        if sides == 1:
+            return []
+        here, there = out_ref.at[0, h, some], out_ref.at[1, h, some]
+        return [remote(here, there, sends.at[at, which], recvs.at[at, which], other)]
 
     outgoing = []
     for h in range(halves):
@@ -399,20 +402,24 @@
         dft_modes(xf, rows, tables)
         spec[h] = pair_lanes(rows[...]).reshape(spec.shape[1:]).astype(HALF)
         outgoing.append(send_spectra(h))
-    for h, (copies, own, passed, at) in enumerate(outgoing):
-        for copy, source, step in copies:
-            copy.wait_recv()
-            if sides > 1:
-                passed.append(
-                    remote(out_ref.at[0, h, source], out_ref.at[1, h, source],
-                           sends.at[at, step], recvs.at[at, step], other)
-                )
-    for copies, own, passed, _ in outgoing:
+    passed = []
+    for h, (copies, own, at) in enumerate(outgoing):
+        pass_at = next(slot)
         own.wait()
-        for copy, _, _ in copies:
+        for r in range(parts // plane):
+            row = partner(me, r * plane) // plane
+            for step in range(r * plane, (r + 1) * plane):
+                if step:
+                    arrived(h, at, step)
+            if h == halves - 1:
+                passed += passing(h, pl.ds(row * plane, plane), pass_at, r)
+        if h < halves - 1:
+            passed += passing(h, pl.ds(0, parts), pass_at, 0)
+    for copies, _, _ in outgoing:
+        for copy in copies:
             copy.wait_send()
-        for copy in passed:
-            copy.wait()
+    for copy in passed:
+        copy.wait()
 
 
 def spectra_of(field, coef, listed, parts, sides):

time: 84.9 us -> 83.7 us (0.986)
  the two profiles are of different devices: /device:TPU:9 before, /device:TPU:0 now
where the time goes in v4:
time: 83.7 us; the launch traced here: 82.9 us
  Pallas kernels  82.9 us (99%)
    pallas_call x1, Pallas kernels, spectra_of(): pl.pallas_call(functools.partial(whole_kernel, parts, sides, cuts), out_s...  79.1 us
    pallas_call x1, Pallas kernels, gram(): pl.pallas_call(functools.partial(gram_kernel, scale), out_shape=jax.Shape...  3.86 us

profile of v4, /device:TPU:0, one launch (start us, length us, event | category | flops | bytes accessed | tf_op | source)
XLA Modules:
  0.0 82.9 jit_solution(11048299659095031774)
XLA Ops:
  0.0 79.1 %shard_map.91.spec_ref = bf16[2,2,16,8,16,128]{5,4,3,2,1,0:T(8,128)(2,1)S(1)} custom-call(bf16[2,16,16384]{2,1,0:T(8,128)(2,1)} %bitcast.2, bf16[64,64]{1,0:T(8,128)(2,1)} %bitcast.3, s32[1,4]{1,0:T(1,128)} %list_ref.1, bf16[256,256]{1,0:T(8,128)(2,1)} %constant.12.clone.refs_0_, bf16[256,256]{1,0:T(8,128)(2,1)} %constant.13.clone.refs_1_, ...), custom_call_target="tpu_custom_call" | custom-call | tf_op jit(solution)/shard_map/pallas_call | solution.py:439
  79.1 3.9 %shard_map.92 = f32[32,2,128,256]{3,2,1,0:T(8,128)} custom-call(bf16[2,2,16,8,16,128]{5,4,3,2,1,0:T(8,128)(2,1)S(1)} %shard_map.91.spec_ref), custom_call_target="tpu_custom_call" | custom-call | tf_op jit(solution)/shard_map/pallas_call | solution.py:591

commit v5 on v4

--- a/solution.py
+++ b/solution.py
@@ -257,6 +257,30 @@
     slot = iter(range(sends.shape[0]))
     column, row_of = me % plane, me // plane
 
+    def columns_ascending():
+        pairs = []
+        for i in range(plane - 1):
+            to = i + (i - column + plane) // plane
+            step, bit = 0, 1
+            while bit < plane:
+                step = step + (to // bit + column // bit) % 2 * bit
+                bit *= 2
+            pairs.append((row_of * plane + to, step))
+        for r in range(1, parts // plane):
+            for k in range(plane):
+                row = partner(me, r * plane) // plane
+                pairs.append((row * plane + k, r * plane + partner(column, k)))
+        return pairs
+
+    targets = columns_ascending()
+
+    def send_to_all(here, there):
+        at = next(slot)
+        return [
+            remote(here(to), there, sends.at[at, step], recvs.at[at, step], {"mode": to})
+            for to, step in targets
+        ]
+
     def send_all(here, there, steps_of=order):
         at = next(slot)
         return [
@@ -307,7 +331,7 @@
 
     def send_stepped(h, first_tile, tiles):
         some = pl.ds(first_tile // 2, tiles // 2)
-        copies = send_all(lambda to: stepped.at[h, to, some], by_mode.at[h, me, some])
+        copies = send_to_all(lambda to: stepped.at[h, to, some], by_mode.at[h, me, some])
         at = own_sems.at[20 + halves * pieces + h if tiles == fine else 20 + h * pieces + starts.index(first_tile)]
         copies.append(local(stepped.at[h, me, some], by_mode.at[h, me, some], at))
         mode_copies[h].append((first_tile, tiles, copies))
@@ -346,23 +370,6 @@
         send_stepped(h, 0, fine)
     for copy in early:
         copy.wait()
-
-    def columns_ascending():
-        pairs = []
-        for i in range(plane - 1):
-            to = i + (i - column + plane) // plane
-            step, bit = 0, 1
-            while bit < plane:
-                step = step + (to // bit + column // bit) % 2 * bit
-                bit *= 2
-            pairs.append((row_of * plane + to, step))
-        for r in range(1, parts // plane):
-            for k in range(plane):
-                row = partner(me, r * plane) // plane
-                pairs.append((row * plane + k, r * plane + partner(column, k)))
-        return pairs
-
-    targets = columns_ascending()
 
     def send_spectra(h):
         at = next(slot)

time: 83.7 us -> 83.8 us (level)
  no operation moved by 1% of the time
where the time goes in v5:
time: 83.8 us; the launch traced here: 83 us
  Pallas kernels  83 us (99%)
    pallas_call x1, Pallas kernels, spectra_of(): pl.pallas_call(functools.partial(whole_kernel, parts, sides, cuts), out_s...  79.1 us
    pallas_call x1, Pallas kernels, gram(): pl.pallas_call(functools.partial(gram_kernel, scale), out_shape=jax.Shape...  3.85 us

profile of v5, /device:TPU:0, one launch (start us, length us, event | category | flops | bytes accessed | tf_op | source)
XLA Modules:
  0.0 83.0 jit_solution(6379638603231343)
XLA Ops:
  0.0 79.1 %shard_map.91.spec_ref = bf16[2,2,16,8,16,128]{5,4,3,2,1,0:T(8,128)(2,1)S(1)} custom-call(bf16[2,16,16384]{2,1,0:T(8,128)(2,1)} %bitcast.2, bf16[64,64]{1,0:T(8,128)(2,1)} %bitcast.3, s32[1,4]{1,0:T(1,128)} %list_ref.1, bf16[256,256]{1,0:T(8,128)(2,1)} %constant.12.clone.refs_0_, bf16[256,256]{1,0:T(8,128)(2,1)} %constant.13.clone.refs_1_, ...), custom_call_target="tpu_custom_call" | custom-call | tf_op jit(solution)/shard_map/pallas_call | solution.py:446
  79.1 3.9 %shard_map.92 = f32[32,2,128,256]{3,2,1,0:T(8,128)} custom-call(bf16[2,2,16,8,16,128]{5,4,3,2,1,0:T(8,128)(2,1)S(1)} %shard_map.91.spec_ref), custom_call_target="tpu_custom_call" | custom-call | tf_op jit(solution)/shard_map/pallas_call | solution.py:598
